TPU v7x, 128 devices: a whole 4x4x4 slice. The times are simulated.
128 devices in a mesh: dp: 4 (over y), seq: 32 (over z, x, core).
Axes of the slice: x: 4, y: 4, z: 4, core: 2. Of those that a mesh axis runs over, the one named last changes fastest.
Arguments:
- queries: bfloat16 [4, 32768, 2048], P('dp', 'seq'), may hold values from -420 to 420
- keys: bfloat16 [4, 32768, 2048], P('dp', 'seq'), may hold values from -24 to 24
- values: bfloat16 [4, 32768, 2048], P('dp', 'seq'), may hold values from -12 to 12
- codes: int32 [4, 16, 32768], P('dp', None, 'seq'), may hold values from 0 to 511
- starts: int32 [4, 64], P('dp', 'seq'), may hold values from 0 to 1
- old_centroids: float32 [16, 512, 128], replicated, may hold values from -6 to 6
- old_counts: float32 [16, 512], replicated, may hold values from 4 to 64
Outputs:
- mixed: bfloat16 [4, 32768, 2048], P('dp', 'seq')
- codebook: float32 [16, 512, 128], P(None, 'dp')
All inputs are finite; a program needn't handle non-finite values.
Results may differ from a plain program's by a relative error of at most 0.0034.
Values sent between devices are 32-bit elements; how exact they have to be, the bound alone decides.
A program may use at most 384 MiB of HBM per device.

v0:
```python
import jax
import jax.numpy as jnp
from jax import lax
from jax.sharding import PartitionSpec as P

HEADS = 16
HEAD_DIM = 128
CODES = 512
BLOCK = 512
TOK_DEV = 1024
RETAIN = 0.9
NEGATIVE = -1e30


def prefix(part, axis, combine, identity):
    place = lax.axis_index(axis)
    gathered = jax.tree.map(lambda a: lax.all_gather(a, axis), part)
    state = jax.tree.map(lambda a, e: jnp.zeros_like(a) + jnp.asarray(e, a.dtype), part, identity)

    def one(hop, state):
        return combine(
            state, jax.tree.map(lambda a: lax.dynamic_index_in_dim(a, hop, 0, False), gathered)
        )

    return lax.fori_loop(0, place, one, state)


def one_hot_rows(code_block):
    return (code_block[:, :, None] == lax.iota(jnp.int32, CODES)[None, None, :]).astype(
        jnp.bfloat16
    )


def refresh_codes(sums, counts, centroids, previous):
    return (RETAIN * previous[..., None] * centroids + (1.0 - RETAIN) * sums) / (
        RETAIN * previous + (1.0 - RETAIN) * counts
    )[..., None]


def join_segments(earlier, later):
    survive = 1.0 - later[2][0]
    return (
        later[0] + survive * earlier[0],
        later[1] + survive * earlier[1],
        jnp.maximum(earlier[2], later[2]),
    )


def shards(queries, keys, values, codes, starts, old_centroids, old_counts):
    blocks_here = TOK_DEV // BLOCK
    flags = starts[0].astype(jnp.float32)
    key_sums = jnp.zeros((HEADS, CODES, HEAD_DIM), jnp.float32)
    code_counts = jnp.zeros((HEADS, CODES), jnp.float32)
    hot_list = []
    value_sums = []
    value_counts = []
    for block_id in range(blocks_here):
        offset = block_id * BLOCK
        hot_table = one_hot_rows(codes[0, :, offset : offset + BLOCK])
        key_part = keys[0, offset : offset + BLOCK].reshape(BLOCK, HEADS, HEAD_DIM)
        value_part = values[0, offset : offset + BLOCK].reshape(BLOCK, HEADS, HEAD_DIM)
        key_sums = key_sums + jnp.einsum(
            "hts,thd->hsd", hot_table, key_part, preferred_element_type=jnp.float32
        )
        counted = jnp.sum(hot_table, axis=1, dtype=jnp.float32)
        code_counts = code_counts + counted
        value_sums.append(
            jnp.einsum("hts,thd->hsd", hot_table, value_part, preferred_element_type=jnp.float32)
        )
        value_counts.append(counted)
        hot_list.append(hot_table)
    total_keys, total_counts = lax.psum((key_sums, code_counts), ("dp", "seq"))
    codebook = refresh_codes(total_keys, total_counts, old_centroids, old_counts)
    code_share = CODES // lax.axis_size("dp")
    codebook_out = lax.dynamic_slice_in_dim(
        codebook, lax.axis_index("dp") * code_share, code_share, 1
    )
    tail_sums = jnp.zeros((HEADS, CODES, HEAD_DIM), jnp.float32)
    tail_counts = jnp.zeros((HEADS, CODES), jnp.float32)
    flag_any = jnp.zeros((1,), jnp.float32)
    for block_id in range(blocks_here):
        survive = 1.0 - flags[block_id]
        tail_sums = survive * tail_sums + value_sums[block_id]
        tail_counts = survive * tail_counts + value_counts[block_id]
        flag_any = jnp.maximum(flag_any, flags[block_id])
    identity = (
        jnp.zeros_like(tail_sums),
        jnp.zeros_like(tail_counts),
        jnp.zeros((1,), jnp.float32),
    )
    enter_sums, enter_counts, ignored_flag = prefix(
        (tail_sums, tail_counts, flag_any), "seq", join_segments, identity
    )
    codebook_half = codebook.astype(jnp.bfloat16)
    score_scale = HEAD_DIM ** (-0.5)
    positions = lax.iota(jnp.int32, BLOCK)
    causal = positions[:, None] >= positions[None, :]
    run_sums = enter_sums
    run_counts = enter_counts
    outputs = []
    for block_id in range(blocks_here):
        offset = block_id * BLOCK
        survive = 1.0 - flags[block_id]
        cache_sums = survive * run_sums
        cache_counts = survive * run_counts
        code_means = (cache_sums / jnp.maximum(cache_counts, 1.0)[..., None]).astype(jnp.bfloat16)
        count_bias = jnp.where(cache_counts > 0, jnp.log(jnp.maximum(cache_counts, 1.0)), NEGATIVE)
        query_part = queries[0, offset : offset + BLOCK].reshape(BLOCK, HEADS, HEAD_DIM)
        value_part = values[0, offset : offset + BLOCK].reshape(BLOCK, HEADS, HEAD_DIM)
        code_scores = (
            jnp.einsum(
                "thd,hsd->hts", query_part, codebook_half, preferred_element_type=jnp.float32
            )
            * score_scale
            + count_bias[:, None, :]
        )
        key_codes = jnp.einsum(
            "hts,hsd->htd", hot_list[block_id], codebook_half, preferred_element_type=jnp.float32
        ).astype(jnp.bfloat16)
        local_scores = jnp.where(
            causal[None],
            jnp.einsum("ihd,hjd->hij", query_part, key_codes, preferred_element_type=jnp.float32)
            * score_scale,
            NEGATIVE,
        )
        row_top = jnp.maximum(jnp.max(code_scores, axis=-1), jnp.max(local_scores, axis=-1))
        code_weights = jnp.exp(code_scores - row_top[..., None])
        local_weights = jnp.where(causal[None], jnp.exp(local_scores - row_top[..., None]), 0.0)
        denominator = jnp.sum(code_weights, axis=-1) + jnp.sum(local_weights, axis=-1)
        mixed_part = jnp.einsum(
            "hts,hsd->htd",
            code_weights.astype(jnp.bfloat16),
            code_means,
            preferred_element_type=jnp.float32,
        )
        mixed_part = mixed_part + jnp.einsum(
            "hij,jhd->hid",
            local_weights.astype(jnp.bfloat16),
            value_part,
            preferred_element_type=jnp.float32,
        )
        out_rows = (
            (mixed_part / denominator[..., None])
            .transpose(1, 0, 2)
            .reshape(BLOCK, HEADS * HEAD_DIM)
            .astype(jnp.bfloat16)
        )
        outputs.append(out_rows)
        run_sums = cache_sums + value_sums[block_id]
        run_counts = cache_counts + value_counts[block_id]
    mixed = jnp.concatenate(outputs, axis=0)[None]
    return (mixed, codebook_out)


def solution(mesh):
    placed = (
        P("dp", "seq", None),
        P("dp", "seq", None),
        P("dp", "seq", None),
        P("dp", None, "seq"),
        P("dp", "seq"),
        P(),
        P(),
    )
    return jax.shard_map(
        shards,
        mesh=mesh,
        in_specs=placed,
        out_specs=(P("dp", "seq", None), P(None, "dp", None)),
        check_vma=False,
    )
```

profile of v0, /device:TPU:103, one launch (start us, length us, event | category | flops | bytes accessed | tf_op | source)
XLA Modules:
  0.0 883.3 jit_solution(4098301958992712305)
XLA Ops:
  8.8 4.0 fusion.78
  12.8 3.9 copy.85
  16.8 2.5 copy.86
  19.2 5.8 fusion.8
  25.0 5.7 fusion.61
  33.3 4.7 convert_reduce_fusion
  38.6 4.0 fusion.77
  42.6 4.0 copy.88
  46.6 2.5 copy.89
  49.1 5.8 fusion.6
  55.0 1.9 copy-done.10
  56.9 5.7 multiply_add_fusion.2
  63.9 4.2 fusion.76
  68.1 4.0 copy.87
  72.1 2.5 copy.90
  75.9 63.2 %all-reduce = f32[32]{0:T(128)S(1)} all-reduce(f32[32]{0:T(128)S(1)} %bitcast_dynamic-update-slice_fusion), channel_id=1, replica_groups=mesh['dp'=4,'seq'=32] {'seq'}, use_global_device_ids=true, to_apply=%add | all-reduce | flops 32 | bytes 256
  139.1 67.3 %psum.15 = f32[16,512]{1,0:T(8,128)S(1)} all-reduce(f32[16,512]{1,0:T(8,128)S(1)} %get-tuple-element.93), channel_id=1, replica_groups=mesh['dp'=4,'seq'=32] {'dp','seq'}, use_global_device_ids=true, to_apply=%region_3.0 | all-reduce | flops 8192 | bytes 65536 | tf_op jit(solution)/shard_map/psum | solution.py:72
  206.6 285.1 %all-reduce.3.cloned.1.call-done = f32[16,512,128]{2,1,0:T(8,128)} async-done(((f32[16,512,128]{2,1,0:T(8,128)}), f32[16,512,128]{2,1,0:T(8,128)}) %all-reduce.3.cloned.1.call-update) | async-done | bytes 4194320 | tf_op jit(solution)/shard_map/psum | solution.py:72
  491.7 5.1 fusion.74
  497.9 10.2 %fusion.14 = (f32[16,512]{1,0:T(8,128)S(1)}, f32[16,512,512]{2,1,0:T(8,128)}) fusion(pred[512,512]{0,1:T(8,128)(4,1)S(1)} %iota_compare_fusion.12, bf16[512,16,128]{0,2,1:T(8,128)(2,1)} %bitcast.107, bf16[16,512,128]{2,1,0:T(8,128)(2,1)S(1)} %get-tuple-element.82, s32[16,512]{1,0:T(8,128)S(1)} %get-tuple-element.95), kind=kOutput, calls=%fused_computation.27 | convolution fusion | flops 2165301248 | bytes 21299200 | tf_op jit(solution)/shard_map/ihd,hjd->hij/dot_general | solution.py:122
  508.1 2.5 broadcast.60
  510.6 261.9 %while.14 = (s32[]{:T(128)}, f32[16,512,128]{2,1,0:T(8,128)}, f32[16,512]{1,0:T(8,128)S(1)}, s32[]{:T(128)}, f32[32,16,512,128]{3,2,1,0:T(8,128)}, /*index=5*/f3...) while((s32[]{:T(128)}, f32[16,512,128]{2,1,0:T(8,128)}, ...), condition=%wide.region_5.6_spmd, body=%wide.region_4.5_spmd.sunk | while | flops 2113542 | bytes 12681379 | solution.py:25
  511.1 6.6 bitcast_add_fusion.4
  519.6 6.6 bitcast_add_fusion.4
  528.0 6.6 bitcast_add_fusion.4
  536.5 6.6 bitcast_add_fusion.4
  544.9 6.6 bitcast_add_fusion.4
  553.4 6.6 bitcast_add_fusion.4
  561.8 6.6 bitcast_add_fusion.4
  570.3 6.6 bitcast_add_fusion.4
  578.7 6.6 bitcast_add_fusion.4
  587.2 6.6 bitcast_add_fusion.4
  595.6 6.6 bitcast_add_fusion.4
  604.1 6.6 bitcast_add_fusion.4
  612.5 6.6 bitcast_add_fusion.4
  621.0 6.6 bitcast_add_fusion.4
  629.4 6.6 bitcast_add_fusion.4
  637.9 6.6 bitcast_add_fusion.4
  646.3 6.6 bitcast_add_fusion.4
  654.8 6.6 bitcast_add_fusion.4
  663.2 6.6 bitcast_add_fusion.4
  671.7 6.6 bitcast_add_fusion.4
  680.1 6.6 bitcast_add_fusion.4
  688.5 6.6 bitcast_add_fusion.4
  697.0 6.6 bitcast_add_fusion.4
  705.4 6.6 bitcast_add_fusion.4
  713.9 6.6 bitcast_add_fusion.4
  722.3 6.6 bitcast_add_fusion.4
  730.8 6.6 bitcast_add_fusion.4
  739.2 6.6 bitcast_add_fusion.4
  747.7 6.6 bitcast_add_fusion.4
  756.1 6.6 bitcast_add_fusion.4
  764.6 6.6 bitcast_add_fusion.4
  772.5 8.2 bitcast_reduce_fusion.1
  780.7 22.1 %fusion.20 = (f32[16,512]{1,0:T(8,128)S(1)}, f32[16,512]{1,0:T(8,128)S(1)}, f32[16,512]{1,0:T(8,128)S(1)}, f32[16,512,512]{2,1,0:T(8,128)}) fusion(f32[16,512,512]{2,1,0:T(8,128)} %get-tuple-element.107, f32[16,512]{1,0:T(8,128)S(1)} %max.29, pred[512,512]{0,1:T(8,128)(4,1)S(1)} %iota_compare_fusion.12, f32[16,512]{1,0:T(8,128)S(1)} %get-tuple-element.97, ...), kind=kOutput, calls=%fused_computation.33 | convolution fusion | flops 2203033600 | bytes 54984704 | tf_op jit(solution)/shard_map/ihd,hjd->hij/dot_general | solution.py:122
  802.8 9.5 %fusion.26 = f32[16,512,128]{1,2,0:T(8,128)S(1)} fusion(f32[16,512,512]{2,1,0:T(8,128)} %get-tuple-element.105, f32[16,512]{1,0:T(8,128)S(1)} %max.29, f32[16,512]{1,0:T(8,128)S(1)} %get-tuple-element.97, f32[16,512,128]{2,1,0:T(8,128)} %get-tuple-element.62, f32[16,512]{1,0:T(8,128)S(1)} %get-tuple-element.96, f32[]{:T(128)} %bitcast.8), kind=kOutput, calls=%fused_computation.38 | convolution fusion | flops 1093664768 | bytes 25264132 | tf_op jit(solution)/shard_map/hts,hsd->htd/dot_general | solution.py:130
  812.4 9.3 %fusion.47 = bf16[512,16,128]{0,2,1:T(8,128)(2,1)} fusion(f32[16,512,128]{1,2,0:T(8,128)S(1)} %fusion.26, f32[512,16]{0,1:T(8,128)S(1)} %add_bitcast_fusion.1, bf16[512,16,128]{0,2,1:T(8,128)(2,1)S(1)} %bitcast.112, f32[16,512,512]{2,1,0:T(8,128)} %get-tuple-element.107, f32[16,512]{1,0:T(8,128)S(1)} %max.29, pred[512,512]{0,1:T(8,128)(4,1)S(1)} %iota_compare_fusion.12), kind=kOutput, calls=%fused_computation.59 | convolution fusion | flops 1097859072 | bytes 25493504 | tf_op jit(solution)/shard_map/hij,jhd->hid/dot_general | solution.py:136
  821.7 4.0 copy.65
  825.7 4.3 bitcast_reduce_fusion
  830.0 16.9 %fusion.22 = (f32[16,512]{1,0:T(8,128)S(1)}, f32[16,512]{1,0:T(8,128)S(1)}) fusion(f32[16,512,512]{2,1,0:T(8,128)} %get-tuple-element.108, f32[16,512]{1,0:T(8,128)S(1)} %max.31, pred[512,512]{0,1:T(8,128)(4,1)S(1)} %iota_compare_fusion.12, f32[16,512]{1,0:T(8,128)S(1)} %get-tuple-element.91, f32[16,512,512]{2,1,0:T(8,128)S(1)} %get-tuple-element.103), kind=kLoop, calls=%fused_computation.35 | loop fusion | flops 37732352 | bytes 33947648 | tf_op jit(solution)/shard_map/reduce_sum | solution.py:129
  846.9 10.3 %fusion.24 = f32[16,512,128]{1,2,0:T(8,128)} fusion(f32[16,512,512]{2,1,0:T(8,128)} %copy-done.1, f32[16,512]{1,0:T(8,128)S(1)} %max.31, f32[16,512]{1,0:T(8,128)S(1)} %get-tuple-element.91, f32[16,512,128]{2,1,0:T(8,128)S(1)} %copy-done.11, f32[16,512,128]{2,1,0:T(8,128)S(1)} %copy-done, f32[16,512]{1,0:T(8,128)S(1)} %get-tuple-element.90, f32[]{:T(128)} %bitcast.8, ...), kind=kOutput, calls=%fused_computation.37 | convolution fusion | flops 1095761920 | bytes 29458440 | tf_op jit(solution)/shard_map/hts,hsd->htd/dot_general | solution.py:130
  857.2 10.3 %fusion.46 = bf16[512,16,128]{0,2,1:T(8,128)(2,1)} fusion(f32[16,512,128]{1,2,0:T(8,128)} %fusion.24, f32[512,16]{0,1:T(8,128)S(1)} %add_bitcast_fusion, bf16[512,16,128]{0,2,1:T(8,128)(2,1)S(1)} %bitcast.110, f32[16,512,512]{2,1,0:T(8,128)} %get-tuple-element.108, f32[16,512]{1,0:T(8,128)S(1)} %max.31, pred[512,512]{0,1:T(8,128)(4,1)S(1)} %iota_compare_fusion.12), kind=kOutput, calls=%fused_computation.57 | convolution fusion | flops 1097859072 | bytes 25493504 | tf_op jit(solution)/shard_map/hij,jhd->hid/dot_general | solution.py:136
  867.6 4.1 copy.66
  871.7 4.2 maximum_bitcast_fusion
  (109 shorter events, 63.8 us)
Async XLA Ops:
  8.0 483.7 %all-reduce.3.cloned.1.call-start = ((), (), s32[]{:S(2)}) async-start(), calls=%async_computation | async-start | bytes 8388608 | tf_op jit(solution)/shard_map/psum | solution.py:72
  19.2 5.8 copy-start.6
  30.7 0.7 copy-start.8
  30.8 477.4 %all-gather.7.cloned.1.call-start = ((), (), s32[]{:S(2)}) async-start(), calls=%async_computation.2 | async-start | bytes 1081344 | tf_op jit(solution)/shard_map/all_gather | solution.py:17
  38.6 469.6 %all-gather.5.cloned.1.call-start = ((), (), s32[]{:S(2)}) async-start(), calls=%async_computation.1 | async-start | bytes 138412032 | tf_op jit(solution)/shard_map/all_gather | solution.py:17
  49.1 7.7 copy-start.3
  54.9 1.9 copy-start.10
  68.1 6.5 copy-start.9
  68.1 138.4 %copy-start.7 = (f32[16,512]{1,0:T(8,128)S(1)}, f32[16,512]{1,0:T(8,128)}, u32[]{:S(2)}) copy-start(f32[16,512]{1,0:T(8,128)} %param.15) | copy-start | bytes 98308
  802.8 9.6 %copy-start.5 = (bf16[1,512,2048]{1,2,0:T(8,128)(2,1)S(1)}, bf16[1,512,2048]{1,2,0:T(8,128)(2,1)}, u32[]{:S(2)}) copy-start(bf16[1,512,2048]{1,2,0:T(8,128)(2,1)} %copy.88) | copy-start | bytes 6291460
  830.0 16.9 %copy-start.1 = (f32[16,512,512]{2,1,0:T(8,128)}, f32[16,512,512]{2,1,0:T(8,128)S(1)}, u32[]{:S(2)}) copy-start(f32[16,512,512]{2,1,0:T(8,128)S(1)} %get-tuple-element.103) | copy-start | bytes 50331652
  830.0 16.9 %copy-start = (f32[16,512,128]{2,1,0:T(8,128)S(1)}, f32[16,512,128]{2,1,0:T(8,128)}, u32[]{:S(2)}) copy-start(f32[16,512,128]{2,1,0:T(8,128)} %get-tuple-element.62) | copy-start | bytes 12582916
  830.0 16.9 %copy-start.11 = (f32[16,512,128]{2,1,0:T(8,128)S(1)}, f32[16,512,128]{2,1,0:T(8,128)}, u32[]{:S(2)}) copy-start(f32[16,512,128]{2,1,0:T(8,128)} %copy-done.10) | copy-start | bytes 12582916
  846.9 10.3 %copy-start.4 = (bf16[1,512,2048]{1,2,0:T(8,128)(2,1)S(1)}, bf16[1,512,2048]{1,2,0:T(8,128)(2,1)}, u32[]{:S(2)}) copy-start(bf16[1,512,2048]{1,2,0:T(8,128)(2,1)} %copy.89) | copy-start | bytes 6291460
  867.6 4.1 copy-start.2
Sparse Core Ops, SparseCore 0:
  30.9 460.7 all-reduce.2
Sparse Core Ops, SparseCore 1:
  38.7 42.5 all-gather.6
  83.9 378.2 all-gather.4
where the time goes:
time: 887 us; the launch traced here: 883 us
  other arithmetic  293 us (33%)
  waiting for transfers between devices  285 us (32%)
  blocking collectives  131 us (15%)
  matrix products  107 us (12%)
  local copies, waits for them, and re-layouts  48.4 us (5%)
  between operations  18.3 us (2%)
    psum x1, waiting for transfers between devices, shards(): total_keys, total_counts = lax.psum((key_sums, code_counts), ('dp', 'seq'))  285 us
    add x31, other arithmetic, join_segments(): later[0] + survive * earlier[0]  203 us
    psum x1, blocking collectives, shards(): total_keys, total_counts = lax.psum((key_sums, code_counts), ('dp', 'seq'))  67.3 us
    unnamed x1, blocking collectives  63.2 us
    add x31, other arithmetic, join_segments(): later[1] + survive * earlier[1]  41.4 us
    dot_general x2, matrix products, shards(): jnp.einsum('ihd,hjd->hij', query_part, key_codes, preferred_element_type=...  32.3 us
    unnamed x33, local copies, waits for them, and re-layouts  23.2 us
    dot_general x2, matrix products, shards(): jnp.einsum('hts,hsd->htd', code_weights.astype(jnp.bfloat16), code_means,...  19.9 us
  transfers between devices with their start and end apart: 3, of which 1 were waited for; matrix products, arithmetic and copies ran while one was open for 6% of the time, Pallas kernels for 0%

commit v1 on v0

--- a/solution.py
+++ b/solution.py
@@ -69,7 +69,7 @@
         )
         value_counts.append(counted)
         hot_list.append(hot_table)
-    total_keys, total_counts = lax.psum((key_sums, code_counts), ("dp", "seq"))
+    total_keys, total_counts = lax.psum(lax.psum((key_sums, code_counts), "dp"), "seq")
     codebook = refresh_codes(total_keys, total_counts, old_centroids, old_counts)
     code_share = CODES // lax.axis_size("dp")
     codebook_out = lax.dynamic_slice_in_dim(

time: 887 us -> 1040 us (1.17)
  waiting for transfers between devices: 285 us -> 433 us
    all_gather x2, waiting for transfers between devices: 0.01 us -> 339 us  [prefix(): gathered = jax.tree.map(lambda a: lax.all_gather(a, axis), part)]
    psum x1 -> x2, waiting for transfers between devices: 285 us -> 94.1 us  [the longest x1 94.1 us: shards(): lax.psum((key_sums, code_counts), 'dp')]
    psum x1 -> x2, blocking collectives: 67.3 us -> 135 us  [the longest x1 124 us: shards(): lax.psum(lax.psum((key_sums, code_counts), 'dp'), 'seq')]
    unnamed x1 -> x0, blocking collectives: 63.2 us -> none
  transfers between devices with their start and end apart: 3 -> 4, of which waited for: 1 -> 2; matrix products, arithmetic and copies ran while one was open for 6% -> 6% of each run, Pallas kernels for 0% -> 0%
where the time goes in v1:
time: 1040 us; the launch traced here: 1030 us
  waiting for transfers between devices  433 us (42%)
  other arithmetic  294 us (28%)
  blocking collectives  135 us (13%)
  matrix products  107 us (10%)
  local copies, waits for them, and re-layouts  47.9 us (5%)
  between operations  16.6 us (2%)
    all_gather x2, waiting for transfers between devices, prefix(): gathered = jax.tree.map(lambda a: lax.all_gather(a, axis), part)  339 us
    add x31, other arithmetic, join_segments(): later[0] + survive * earlier[0]  203 us
    psum x1, blocking collectives, shards(): lax.psum(lax.psum((key_sums, code_counts), 'dp'), 'seq')  124 us
    psum x1, waiting for transfers between devices, shards(): lax.psum((key_sums, code_counts), 'dp')  94.1 us
    add x31, other arithmetic, join_segments(): later[1] + survive * earlier[1]  41.4 us
    dot_general x2, matrix products, shards(): jnp.einsum('ihd,hjd->hij', query_part, key_codes, preferred_element_type=...  32.3 us
    unnamed x33, local copies, waits for them, and re-layouts  22.8 us
  transfers between devices with their start and end apart: 4, of which 2 were waited for; matrix products, arithmetic and copies ran while one was open for 6% of the time, Pallas kernels for 0%

profile of v1, /device:TPU:103, one launch (start us, length us, event | category | flops | bytes accessed | tf_op | source)
XLA Modules:
  0.0 1034.8 jit_solution(2718840360308776661)
XLA Ops:
  8.0 4.0 fusion.78
  12.0 3.9 copy.85
  15.9 2.5 copy.86
  18.4 5.8 fusion.8
  24.2 5.7 fusion.61
  30.0 94.1 %all-reduce.5.cloned.1.call-done = f32[16,512,128]{2,1,0:T(8,128)} async-done(((f32[16,512,128]{2,1,0:T(8,128)}), f32[16,512,128]{2,1,0:T(8,128)}) %all-reduce.5.cloned.1.call-update) | async-done | bytes 4194320 | tf_op jit(solution)/shard_map/psum | solution.py:72
  126.0 4.7 convert_reduce_fusion
  131.4 4.0 fusion.77
  135.4 4.2 copy.88
  139.6 2.5 copy.89
  142.1 5.8 fusion.6
  149.8 5.7 multiply_add_fusion.2
  156.9 4.1 fusion.76
  161.0 4.0 copy.87
  165.0 2.5 copy.90
  168.8 11.6 %psum.30 = f32[16,512]{1,0:T(8,128)S(1)} all-reduce(f32[16,512]{1,0:T(8,128)S(1)} %get-tuple-element.95), channel_id=1, replica_groups=mesh['dp'=4,'seq'=32] {'dp'}, use_global_device_ids=true, to_apply=%region_4.0 | all-reduce | flops 8192 | bytes 65536 | tf_op jit(solution)/shard_map/psum | solution.py:72
  180.4 123.7 %all-reduce.1 = (f32[16,512]{1,0:T(8,128)S(1)}, f32[32]{0:T(128)S(1)}) all-reduce(f32[16,512]{1,0:T(8,128)S(1)} %psum.30, f32[32]{0:T(128)S(1)} %bitcast_dynamic-update-slice_fusion), channel_id=1, replica_groups=mesh['dp'=4,'seq'=32] {'seq'}, use_global_device_ids=true, to_apply=%region_5.0 | all-reduce | flops 8224 | bytes 65792 | tf_op jit(solution)/shard_map/psum | solution.py:72
  304.3 5.8 fusion.74
  311.1 10.3 fusion.14
  321.4 339.3 %all-gather.5.cloned.1.call-done = f32[512,512,128]{2,1,0:T(8,128)} async-done(((f32[16,512,128]{2,1,0:T(8,128)}), f32[512,512,128]{2,1,0:T(8,128)}) %all-gather.5.cloned.1.call-update) | async-done | bytes 134217744 | tf_op jit(solution)/shard_map/all_gather | solution.py:17
  660.7 2.5 broadcast.60
  663.1 261.9 %while.14 = (s32[]{:T(128)}, f32[16,512,128]{2,1,0:T(8,128)}, f32[16,512]{1,0:T(8,128)S(1)}, s32[]{:T(128)}, f32[32,16,512,128]{3,2,1,0:T(8,128)}, /*index=5*/f3...) while((s32[]{:T(128)}, f32[16,512,128]{2,1,0:T(8,128)}, ...), condition=%wide.region_7.8_spmd, body=%wide.region_6.7_spmd.sunk | while | flops 2113542 | bytes 12681379 | solution.py:25
  663.7 6.6 bitcast_add_fusion.4
  672.1 6.6 bitcast_add_fusion.4
  680.6 6.6 bitcast_add_fusion.4
  689.0 6.6 bitcast_add_fusion.4
  697.5 6.6 bitcast_add_fusion.4
  705.9 6.6 bitcast_add_fusion.4
  714.3 6.6 bitcast_add_fusion.4
  722.8 6.6 bitcast_add_fusion.4
  731.2 6.6 bitcast_add_fusion.4
  739.7 6.6 bitcast_add_fusion.4
  748.1 6.6 bitcast_add_fusion.4
  756.6 6.6 bitcast_add_fusion.4
  765.0 6.6 bitcast_add_fusion.4
  773.5 6.6 bitcast_add_fusion.4
  781.9 6.6 bitcast_add_fusion.4
  790.4 6.6 bitcast_add_fusion.4
  798.8 6.6 bitcast_add_fusion.4
  807.3 6.6 bitcast_add_fusion.4
  815.7 6.6 bitcast_add_fusion.4
  824.2 6.6 bitcast_add_fusion.4
  832.6 6.6 bitcast_add_fusion.4
  841.1 6.6 bitcast_add_fusion.4
  849.5 6.6 bitcast_add_fusion.4
  858.0 6.6 bitcast_add_fusion.4
  866.4 6.6 bitcast_add_fusion.4
  874.9 6.6 bitcast_add_fusion.4
  883.3 6.6 bitcast_add_fusion.4
  891.8 6.6 bitcast_add_fusion.4
  900.2 6.6 bitcast_add_fusion.4
  908.6 6.6 bitcast_add_fusion.4
  917.1 6.6 bitcast_add_fusion.4
  925.0 8.2 bitcast_reduce_fusion.1
  933.3 22.1 %fusion.20 = (f32[16,512]{1,0:T(8,128)S(1)}, f32[16,512]{1,0:T(8,128)S(1)}, f32[16,512]{1,0:T(8,128)S(1)}, f32[16,512,512]{2,1,0:T(8,128)}) fusion(f32[16,512,512]{2,1,0:T(8,128)} %get-tuple-element.109, f32[16,512]{1,0:T(8,128)S(1)} %max.29, pred[512,512]{0,1:T(8,128)(4,1)S(1)} %iota_compare_fusion.12, f32[16,512]{1,0:T(8,128)S(1)} %get-tuple-element.99, ...), kind=kOutput, calls=%fused_computation.33 | convolution fusion | flops 2203033600 | bytes 54984704 | tf_op jit(solution)/shard_map/ihd,hjd->hij/dot_general | solution.py:122
  955.3 9.5 fusion.26
  964.9 9.3 fusion.47
  974.2 4.0 copy.65
  978.2 4.3 bitcast_reduce_fusion
  982.5 16.7 %fusion.22 = (f32[16,512]{1,0:T(8,128)S(1)}, f32[16,512]{1,0:T(8,128)S(1)}) fusion(f32[16,512,512]{2,1,0:T(8,128)} %get-tuple-element.110, f32[16,512]{1,0:T(8,128)S(1)} %max.31, pred[512,512]{0,1:T(8,128)(4,1)S(1)} %iota_compare_fusion.12, f32[16,512]{1,0:T(8,128)S(1)} %get-tuple-element.93, f32[16,512,512]{2,1,0:T(8,128)S(1)} %get-tuple-element.105), kind=kLoop, calls=%fused_computation.35 | loop fusion | flops 37732352 | bytes 33947648 | tf_op jit(solution)/shard_map/reduce_sum | solution.py:129
  999.3 10.3 fusion.24
  1009.6 10.3 fusion.46
  1019.9 4.1 copy.66
  1024.1 4.2 maximum_bitcast_fusion
  (112 shorter events, 65.2 us)
Async XLA Ops:
  7.2 116.9 %all-reduce.5.cloned.1.call-start = ((), (), s32[]{:S(2)}) async-start(), calls=%async_computation | async-start | bytes 8388608 | tf_op jit(solution)/shard_map/psum | solution.py:72
  18.4 5.8 copy-start.6
  29.9 94.3 %copy-start.8 = (s32[1,2]{1,0:T(1,128)S(1)}, s32[1,2]{1,0:T(1,128)}, u32[]{:S(2)}) copy-start(s32[1,2]{1,0:T(1,128)} %param.13) | copy-start | bytes 28
  29.9 274.4 %all-reduce.7.cloned.1.call-start = ((), (), s32[]{:S(2)}) async-start(), calls=%async_computation.1 | async-start | bytes 8388608 | tf_op jit(solution)/shard_map/psum | solution.py:72
  124.1 197.3 %all-gather.7.cloned.1.call-start = ((), (), s32[]{:S(2)}) async-start(), calls=%async_computation.3 | async-start | bytes 1081344 | tf_op jit(solution)/shard_map/all_gather | solution.py:17
  131.4 529.3 %all-gather.5.cloned.1.call-start = ((), (), s32[]{:S(2)}) async-start(), calls=%async_computation.2 | async-start | bytes 138412032 | tf_op jit(solution)/shard_map/all_gather | solution.py:17
  142.1 7.7 copy-start.3
  147.9 1.9 copy-start.10
  161.0 6.5 copy-start.9
  161.0 143.2 %copy-start.7 = (f32[16,512]{1,0:T(8,128)S(1)}, f32[16,512]{1,0:T(8,128)}, u32[]{:S(2)}) copy-start(f32[16,512]{1,0:T(8,128)} %param.15) | copy-start | bytes 98308
  955.3 9.6 copy-start.5
  982.5 16.8 %copy-start.1 = (f32[16,512,512]{2,1,0:T(8,128)}, f32[16,512,512]{2,1,0:T(8,128)S(1)}, u32[]{:S(2)}) copy-start(f32[16,512,512]{2,1,0:T(8,128)S(1)} %get-tuple-element.105) | copy-start | bytes 50331652
  982.5 16.7 %copy-start = (f32[16,512,128]{2,1,0:T(8,128)S(1)}, f32[16,512,128]{2,1,0:T(8,128)}, u32[]{:S(2)}) copy-start(f32[16,512,128]{2,1,0:T(8,128)} %get-tuple-element.62) | copy-start | bytes 12582916
  982.5 16.7 %copy-start.11 = (f32[16,512,128]{2,1,0:T(8,128)S(1)}, f32[16,512,128]{2,1,0:T(8,128)}, u32[]{:S(2)}) copy-start(f32[16,512,128]{2,1,0:T(8,128)} %copy-done.10) | copy-start | bytes 12582916
  999.3 10.3 copy-start.4
  1019.9 4.1 copy-start.2
Sparse Core Ops, SparseCore 0:
  30.0 94.0 all-reduce.4
  127.8 110.5 all-reduce.6
  241.0 41.5 all-gather.6
  285.5 375.1 all-gather.4
